TPU v7x, 256 devices: a whole 4x4x8 slice. The times are simulated.
256 devices in a mesh: grp: 32 (over x_hi, z, core), dist: 8 (over y, x_lo).
Axes of the slice: x: 4 (x_hi: 2, x_lo: 2; x = x_hi * 2 + x_lo), y: 4, z: 8, core: 2. Of those that a mesh axis runs over, the one named last changes fastest.
Arguments:
- orbitals: bfloat16 [32, 64, 4096], P('grp', 'dist'), may hold values from -6 to 6
- occupations: bfloat16 [32], P('grp'), may hold values from 0.19921875 to 1
Outputs:
- exchange_action: float32 [32, 64, 4096], P('grp', 'dist')
All inputs are finite; a program needn't handle non-finite values.
Results may differ from a plain program's by a relative error of at most 0.0003.
Values may be sent and summed in bfloat16 or wider, within the bound.
No kernel may reach another device: no remote copies, remote signals or barrier semaphores. Data moves between devices by JAX's collectives and lax.ppermute only.
A program may use at most 64 MiB of HBM per device.

v0:
```python
import math

import jax
import jax.numpy as jnp
from jax import lax
from jax.sharding import PartitionSpec as P

GRID = 64


box_length = 7.0
highest = lax.Precision.HIGHEST


def sent_to_all(x, axis):
    copies = jnp.broadcast_to(x, (lax.axis_size(axis), *x.shape))
    return lax.all_to_all(copies, axis, split_axis=0, concat_axis=0, tiled=True)


def in_order(pieces, dim):
    pieces = jnp.moveaxis(pieces, 0, dim)
    dims = pieces.shape
    return pieces.reshape(*dims[:dim], dims[dim] * dims[dim + 1], *dims[dim + 2 :])


def collect(x, axis, dim):
    pieces = sent_to_all(x, axis)
    return in_order(pieces, dim)


def in_blocks(x, dim, size):
    dims = x.shape
    pieces = x.reshape(*dims[:dim], size, dims[dim] // size, *dims[dim + 1 :])
    return jnp.moveaxis(pieces, dim, 0)


def sent_and_summed(x, axis, dim):
    pieces = in_blocks(x, dim, lax.axis_size(axis))
    arrived = lax.all_to_all(pieces, axis, split_axis=0, concat_axis=0, tiled=True)
    return arrived.sum(axis=0)


def cas_table(length):
    position = jnp.arange(length, dtype=jnp.int32)
    product_index = position[:, None] * position[None, :] % length
    angles = product_index.astype(jnp.float32) * (2.0 * math.pi / length)
    return jnp.cos(angles) + jnp.sin(angles)


def wave_squares(length):
    position = jnp.arange(length, dtype=jnp.int32)
    folded = jnp.minimum(position, length - position)
    return (folded * folded).astype(jnp.float32)


def pair_action(local, local_occ, visit, visit_occ, left, right, reverse_weight, solver):
    near = jnp.take(local, left, axis=0).astype(jnp.float32)
    remote = jnp.take(visit, right, axis=0).astype(jnp.float32)
    potential = solver(near * remote)
    remote_weight = jnp.take(visit_occ, right).astype(jnp.float32)
    near_weight = jnp.take(local_occ, left).astype(jnp.float32) * reverse_weight
    toward = potential * remote * remote_weight[:, None, None]
    backward = potential * near * near_weight[:, None, None]
    members = jnp.arange(local.shape[0], dtype=jnp.int32)
    pick_left = (left[:, None] == members[None, :]).astype(jnp.float32)
    pick_right = (right[:, None] == members[None, :]).astype(jnp.float32)
    to_local = jnp.einsum("pr,pxc->rxc", pick_left, toward, precision=highest)
    to_visit = jnp.einsum("pr,pxc->rxc", pick_right, backward, precision=highest)
    return (to_local, to_visit)


def body(orbitals, occupations):
    members = orbitals.shape[0]
    planes = orbitals.shape[1]
    table = cas_table(GRID)
    squares = wave_squares(GRID)
    coupling = box_length**2 / (math.pi * GRID**3)
    groups = lax.axis_size("grp")
    reach = groups // 2
    rank = lax.axis_index("grp")
    first_left = jnp.array(
        [
            lower_id
            for lower_id in range(members)
            for upper_id in range(members)
            if lower_id <= upper_id
        ],
        jnp.int32,
    )
    first_right = jnp.array(
        [
            upper_id
            for lower_id in range(members)
            for upper_id in range(members)
            if lower_id <= upper_id
        ],
        jnp.int32,
    )
    first_reverse = (first_left < first_right).astype(jnp.float32)
    every_left = jnp.repeat(jnp.arange(members, dtype=jnp.int32), members)
    every_right = jnp.tile(jnp.arange(members, dtype=jnp.int32), members)
    every_reverse = jnp.ones((members * members,), jnp.float32)
    lower_side = rank < reach
    last_scale = lower_side.astype(jnp.float32)
    lanes = lax.axis_size("dist")
    lane = lax.axis_index("dist")
    slots = reach // lanes
    totals = squares[:, None, None] + squares[None, :, None] + squares[None, None, :]
    kernel_full = jnp.where(totals > 0.5, coupling / jnp.maximum(totals, 1.0), 0.0)

    def full_solver(density):
        pair_count = density.shape[0]
        field = density.reshape(pair_count, GRID, GRID, GRID)
        field = jnp.einsum("pxyz,wz->pxyw", field, table, precision=highest)
        field = jnp.einsum("pxyz,vy->pxvz", field, table, precision=highest)
        field = jnp.einsum("pxyz,kx->pkyz", field, table, precision=highest)
        field = field * kernel_full
        field = jnp.einsum("pkyz,xk->pxyz", field, table, precision=highest)
        field = jnp.einsum("pxyz,vy->pxvz", field, table, precision=highest)
        field = jnp.einsum("pxyz,wz->pxyw", field, table, precision=highest)
        return field.reshape(pair_count, GRID, GRID * GRID)

    own = collect(orbitals, "dist", 1)
    spread, spread_occ = (
        lax.all_gather(orbitals, "grp", axis=0, tiled=True),
        lax.all_gather(occupations, "grp", axis=0, tiled=True),
    )
    offsets = (
        jnp.arange(lanes, dtype=jnp.int32)[:, None] * slots
        + jnp.arange(slots, dtype=jnp.int32)[None, :]
        + 1
    )
    sources = (rank - offsets) % groups
    stacked = spread.reshape(groups, members, planes, GRID * GRID)
    outgoing = jnp.take(stacked, sources, axis=0)
    arrived = lax.all_to_all(outgoing, "dist", split_axis=0, concat_axis=3, tiled=True)
    guests = arrived.reshape(slots, members, GRID, GRID * GRID)
    mine = lax.dynamic_index_in_dim(sources, lane, 0, keepdims=False)
    guest_occ = jnp.take(spread_occ.reshape(groups, members), mine, axis=0)

    def slot_step(slot, carry):
        summed, terms = carry
        visit = lax.dynamic_index_in_dim(guests, slot, 0, keepdims=False)
        visit_occ = lax.dynamic_index_in_dim(guest_occ, slot, 0, keepdims=False)
        to_local, to_visit = pair_action(
            own, occupations, visit, visit_occ, every_left, every_right, every_reverse, full_solver
        )
        terms = lax.dynamic_update_index_in_dim(terms, to_visit, slot, 0)
        return (summed + to_local, terms)

    start = (
        jnp.zeros((members, GRID, GRID * GRID), jnp.float32),
        jnp.zeros((slots, members, GRID, GRID * GRID), jnp.float32),
    )
    summed, terms = lax.fori_loop(0, slots - 1, slot_step, start)
    final_visit = guests[slots - 1]
    final_occ = guest_occ[slots - 1]

    def ordinary_slot():
        return pair_action(
            own,
            occupations,
            final_visit,
            final_occ,
            every_left,
            every_right,
            every_reverse,
            full_solver,
        )

    def closing_slot():
        halfway = pair_action(
            own,
            occupations,
            final_visit,
            final_occ,
            every_left,
            every_right,
            every_reverse,
            full_solver,
        )
        inner = pair_action(
            own, occupations, own, occupations, first_left, first_right, first_reverse, full_solver
        )
        return (halfway[0] * last_scale + inner[0] + inner[1], halfway[1] * last_scale)

    to_local, to_visit = lax.cond(lane == lanes - 1, closing_slot, ordinary_slot)
    summed = summed + to_local
    terms = terms.at[slots - 1].set(to_visit)
    own_part = sent_and_summed(summed, "dist", 1)
    moved = lax.all_to_all(terms, "dist", split_axis=2, concat_axis=0, tiled=True)
    ordered = jnp.flip(moved, axis=0)
    padded = jnp.concatenate(
        [ordered, jnp.zeros((groups - reach,) + ordered.shape[1:], jnp.float32)], axis=0
    )
    placed = jnp.roll(padded, rank - reach, axis=0)
    returned = lax.psum_scatter(
        placed.reshape(groups * members, planes, GRID * GRID),
        "grp",
        scatter_dimension=0,
        tiled=True,
    )
    return -(own_part + returned)


def solution(mesh):
    in_specs = (P("grp", "dist", None), P("grp"))
    out_specs = P("grp", "dist", None)
    return jax.shard_map(body, mesh=mesh, in_specs=in_specs, out_specs=out_specs, check_vma=False)
```

profile of v0, /device:TPU:8, one launch (start us, length us, event | category | flops | bytes accessed | tf_op | source)
XLA Modules:
  0.0 437.6 jit_solution(2976893758733831661)
XLA Ops:
  8.9 5.8 %all-to-all-start = ((bf16[8,1,8,4096]{3,2,1,0:T(8,128)(2,1)}), bf16[8,1,8,4096]{3,2,1,0:T(8,128)(2,1)S(1)}, u32[]{:S(2)}, u32[]{:S(2)}) async-start(bf16[8,1,8,4096]{3,2,1,0:T(8,128)(2,1)} %broadcast_in_dim.108), calls=%async_computation | async-start | bytes 1048576 | tf_op jit(solution)/shard_map/all_to_all | solution.py:17
  17.6 72.2 %all-reduce = bf16[32]{0:T(256)(128)(2,1)S(1)} all-reduce(bf16[32]{0:T(256)(128)(2,1)S(1)} %dynamic-update-slice.3), channel_id=1, replica_groups=mesh['grp'=32,'dist'=8] {'grp'}, use_global_device_ids=true, to_apply=%add | all-reduce | flops 32 | bytes 128
  96.2 4.8 %all-to-all-start.1 = ((bf16[8,2,1,8,4096]{4,3,1,2,0:T(8,128)(2,1)}), bf16[8,2,1,8,4096]{4,3,1,2,0:T(8,128)(2,1)}, u32[]{:S(2)}, u32[]{:S(2)}) async-start(bf16[8,2,1,8,4096]{4,3,1,2,0:T(8,128)(2,1)} %broadcast_select_fusion), calls=%async_computation.1 | async-start | bytes 2097152 | tf_op jit(solution)/shard_map/all_to_all | solution.py:136
  105.6 9.8 %all-to-all-done.1 = bf16[8,2,1,8,4096]{4,3,1,2,0:T(8,128)(2,1)} async-done(((bf16[8,2,1,8,4096]{4,3,1,2,0:T(8,128)(2,1)}), bf16[8,2,1,8,4096]{4,3,1,2,0:T(8,128)(2,1)}, u32[]{:S(2)}, u32[]{:S(2)}) %all-to-all-start.1) | async-done | bytes 1048608 | tf_op jit(solution)/shard_map/all_to_all | solution.py:136
  120.7 4.5 %fusion.58 = f32[64,64,64]{2,1,0:T(8,128)S(1)} fusion(f32[64,64,64]{2,1,0:T(8,128)} %reshape.713, f32[64,64,64]{2,1,0:T(8,128)} %reshape.714), kind=kOutput, calls=%fused_computation.78 | convolution fusion | flops 201650176 | bytes 3145728 | tf_op jit(solution)/shard_map/while/body/eval_jaxpr/pxyz,wz->pxyw/dot_general | solution.py:114
  127.4 3.1 fusion.54
  133.0 3.1 fusion.52
  136.2 3.7 multiply_multiply_fusion.4
  139.9 17.5 %broadcast_in_dim.114 = f32[1,1,64,4096]{3,1,0,2:T(1,128)} reshape(f32[64,64,64]{2,1,0:T(8,128)} %get-tuple-element.277) | data formatting | bytes 2097152 | tf_op jit(solution)/shard_map/while/body/eval_jaxpr/jit(dynamic_update_index_in_dim)/broadcast_in_dim | solution.py:148
  157.5 63.1 %conditional.1 = (f32[1,64,4096]{2,1,0:T(8,128)S(1)}, f32[1,1,64,4096]{3,1,0,2:T(1,128)}) conditional(s32[]{:T(128)} %convert_element_type.206, (bf16[1,64,4096]{2,1,0:T(8,128)(2,1)S(1)}, bf16[1,64,4096]{2,1,0:T(8,128)(2,1)S(1)}, f32[64,64]{1,0:T(8,128)S(1)}, f32[64,64]{1,0:T(8,128)S(1)}, f32[64,64]{1,0:T(8,128)S(1)}, ...), branch_computations={%region_0.1_spmd, %region_1.2_spmd.clone} | conditional | flops 2420375552 | bytes 62062712 | solution.py:187
  162.0 8.3 %fusion.3 = f32[64,64,64]{1,2,0:T(8,128)S(1)} fusion(f32[64,64,64]{2,1,0:T(8,128)} %reshape.692, f32[64,64,64]{2,1,0:T(8,128)} %reshape.693, f32[64,64]{1,0:T(8,128)S(1)} %get-tuple-element.105), kind=kOutput, calls=%fused_computation.8 | convolution fusion | flops 201588736 | bytes 3162112 | tf_op jit(solution)/shard_map/cond/branch_0_fun/pxyz,wz->pxyw/dot_general | solution.py:114
  170.3 3.2 convolution_bitcast_fusion
  173.5 4.2 copy.58
  177.7 4.8 %fusion.10 = f32[64,64,64]{2,1,0:T(8,128)} fusion(f32[64,64,64]{0,2,1:T(8,128)} %copy.58, f32[64,64]{1,0:T(8,128)S(1)} %get-tuple-element.105), kind=kOutput, calls=%fused_computation.16 | convolution fusion | flops 201326592 | bytes 2113536 | tf_op jit(solution)/shard_map/cond/branch_0_fun/pxyz,kx->pkyz/dot_general | solution.py:116
  184.3 3.8 fusion.5
  188.1 3.1 copy.59
  191.3 4.9 %fusion.7 = f32[64,64,64]{2,1,0:T(8,128)} fusion(f32[64,64,64]{1,2,0:T(8,128)} %copy.59, f32[64,64]{1,0:T(8,128)S(1)} %get-tuple-element.105), kind=kOutput, calls=%fused_computation.13 | convolution fusion | flops 201326592 | bytes 2113536 | tf_op jit(solution)/shard_map/cond/branch_0_fun/pxyz,vy->pxvz/dot_general | solution.py:119
  197.5 7.6 %multiply_multiply_fusion = (f32[64,64,64]{2,1,0:T(8,128)}, f32[64,64,64]{2,1,0:T(8,128)}) fusion(f32[64,64,64]{2,1,0:T(8,128)S(1)} %copy-done.2, f32[]{:T(128)S(6)} %convert.30, f32[]{:T(128)S(6)} %convert.29, f32[64,64,64]{2,1,0:T(8,128)} %reshape.693, f32[64,64]{1,0:T(8,128)S(1)} %get-tuple-element.105, f32[64,64,64]{2,1,0:T(8,128)} %fusion.7), kind=kOutput, calls=%fused_computation.6 | convolution fusion | flops 202375168 | bytes 5259272 | tf_op jit(solution)/shard_map/cond/branch_0_fun/pxyz,wz->pxyw/dot_general | solution.py:120
  220.6 5.5 %pad_maximum_fusion = f32[2,1,64,4096]{3,1,0,2:T(1,128)} fusion(f32[1,1,64,4096]{3,1,0,2:T(1,128)} %get-tuple-element.233, f32[1,1,64,4096]{3,1,0,2:T(1,128)} %broadcast_in_dim.114), kind=kLoop, calls=%fused_computation.66 | loop fusion | flops 524288 | bytes 4194304 | tf_op jit(solution)/shard_map/scatter | solution.py:189
  226.1 42.8 %all-to-all-start.3 = ((f32[2,1,64,4096]{3,1,0,2:T(1,128)}), f32[2,1,64,4096]{3,1,0,2:T(1,128)S(1)}, u32[]{:S(2)}, u32[]{:S(2)}) async-start(f32[2,1,64,4096]{3,1,0,2:T(1,128)} %pad_maximum_fusion), calls=%async_computation.3 | async-start | bytes 4194304 | tf_op jit(solution)/shard_map/all_to_all | solution.py:191
  268.9 25.4 %all-to-all-done.3 = f32[2,1,64,4096]{3,1,0,2:T(1,128)S(1)} async-done(((f32[2,1,64,4096]{3,1,0,2:T(1,128)}), f32[2,1,64,4096]{3,1,0,2:T(1,128)S(1)}, u32[]{:S(2)}, u32[]{:S(2)}) %all-to-all-start.3) | async-done | bytes 2097184 | tf_op jit(solution)/shard_map/all_to_all | solution.py:191
  299.2 4.3 fusion.47
  308.1 18.4 %all_to_all.43 = f32[8,1,8,4096]{3,2,1,0:T(8,128)S(1)} all-to-all(f32[8,1,8,4096]{3,2,1,0:T(8,128)S(1)} %add_bitcast_fusion), channel_id=1, replica_groups=mesh['grp'=32,'dist'=8] {'dist'}, dimensions={0} | all-to-all | bytes 2097152 | tf_op jit(solution)/shard_map/all_to_all | solution.py:39
  326.5 102.5 %reduce-scatter.2.cloned.1.call-done = f32[1,8,4096]{2,1,0:T(8,128)} async-done(((f32[32,8,4096]{2,1,0:T(8,128)}), f32[1,8,4096]{2,1,0:T(8,128)}) %reduce-scatter.2.cloned.1.call-update) | async-done | bytes 131088 | tf_op jit(solution)/shard_map/reduce_scatter | solution.py:197
  (57 shorter events, 46.8 us)
Async XLA Ops:
  6.5 86.3 %all-gather.2.cloned.1.call-start = ((), (), s32[]{:S(2)}) async-start(), calls=%async_computation.5 | async-start | bytes 2162688 | tf_op jit(solution)/shard_map/all_gather | solution.py:125
  8.9 87.3 %all-to-all-start = ((bf16[8,1,8,4096]{3,2,1,0:T(8,128)(2,1)}), bf16[8,1,8,4096]{3,2,1,0:T(8,128)(2,1)S(1)}, u32[]{:S(2)}, u32[]{:S(2)}) async-start(bf16[8,1,8,4096]{3,2,1,0:T(8,128)(2,1)} %broadcast_in_dim.108), calls=%async_computation | async-start | bytes 1048576 | tf_op jit(solution)/shard_map/all_to_all | solution.py:17
  96.2 19.1 %all-to-all-start.1 = ((bf16[8,2,1,8,4096]{4,3,1,2,0:T(8,128)(2,1)}), bf16[8,2,1,8,4096]{4,3,1,2,0:T(8,128)(2,1)}, u32[]{:S(2)}, u32[]{:S(2)}) async-start(bf16[8,2,1,8,4096]{4,3,1,2,0:T(8,128)(2,1)} %broadcast_select_fusion), calls=%async_computation.1 | async-start | bytes 2097152 | tf_op jit(solution)/shard_map/all_to_all | solution.py:136
  133.0 3.1 copy-start.1
  133.0 3.1 copy-start.3
  191.3 6.2 %copy-start.2 = (f32[64,64,64]{2,1,0:T(8,128)S(1)}, f32[64,64,64]{2,1,0:T(8,128)}, u32[]{:S(2)}) copy-start(f32[64,64,64]{2,1,0:T(8,128)} %reshape.692) | copy-start | bytes 3145732 | tf_op jit(solution)/shard_map/cond
  205.1 2.3 copy-start.6
  226.1 68.2 %all-to-all-start.3 = ((f32[2,1,64,4096]{3,1,0,2:T(1,128)}), f32[2,1,64,4096]{3,1,0,2:T(1,128)S(1)}, u32[]{:S(2)}, u32[]{:S(2)}) async-start(f32[2,1,64,4096]{3,1,0,2:T(1,128)} %pad_maximum_fusion), calls=%async_computation.3 | async-start | bytes 4194304 | tf_op jit(solution)/shard_map/all_to_all | solution.py:191
  268.9 160.1 %reduce-scatter.2.cloned.1.call-start = ((), (), s32[]{:S(2)}) async-start(), calls=%async_computation.6 | async-start | bytes 4325376 | tf_op jit(solution)/shard_map/reduce_scatter | solution.py:197
  297.6 1.6 copy-start.7
  303.5 1.6 copy-start.5
Sparse Core Ops, SparseCore 0:
  10.1 82.6 all-gather.1
  303.7 125.3 reduce-scatter.1
where the time goes:
time: 443 us; the launch traced here: 438 us
  waiting for transfers between devices  141 us (32%)
  blocking collectives  90.6 us (20%)
  local copies, waits for them, and re-layouts  56.5 us (13%)
  starting transfers between devices  53.5 us (12%)
  matrix products  51.7 us (12%)
  other arithmetic  17.4 us (4%)
  between operations  15.1 us (3%)
  loops' own time  12.3 us (3%)
    reduce_scatter x1, waiting for transfers between devices, body(): lax.psum_scatter(placed.reshape(groups * members, planes, GRID * GRID), '...  102 us
    unnamed x1, blocking collectives  72.2 us
    all_to_all x1, starting transfers between devices, body(): lax.all_to_all(terms, 'dist', split_axis=2, concat_axis=0, tiled=True)  42.8 us
    all_to_all x1, waiting for transfers between devices, body(): lax.all_to_all(terms, 'dist', split_axis=2, concat_axis=0, tiled=True)  25.4 us
    dot_general x4, matrix products, full_solver(): field = jnp.einsum('pxyz,wz->pxyw', field, table, precision=highest)  24.2 us
    all_to_all x1, blocking collectives, sent_and_summed(): lax.all_to_all(pieces, axis, split_axis=0, concat_axis=0, tiled=True)  18.4 us
    broadcast_in_dim x1, local copies, waits for them, and re-layouts, slot_step(): terms = lax.dynamic_update_index_in_dim(terms, to_visit, slot, 0)  17.5 us
    dot_general x4, matrix products, full_solver(): field = jnp.einsum('pxyz,vy->pxvz', field, table, precision=highest)  13.3 us
  transfers between devices with their start and end apart: 5, of which 4 were waited for; matrix products, arithmetic and copies ran while one was open for 3% of the time, Pallas kernels for 0%

commit v1 on v0

v1 whole, which is shorter than its diff:
```python
import math

import jax
import jax.numpy as jnp
import numpy as np
from jax import lax
from jax.experimental import pallas as pl
from jax.experimental.pallas import tpu as pltpu
from jax.sharding import PartitionSpec as P
GRID = 64
GF = 8
GM = 8
box_length = 7.0

def split(x):
    hi = x.astype(jnp.bfloat16)
    lo = (x - hi.astype(jnp.float32)).astype(jnp.bfloat16)
    return hi, lo

def tables():
    position = np.arange(GRID)
    angles = (position[:, None] * position[None, :] % GRID) * (2.0 * math.pi / GRID)
    t = np.cos(angles) + np.sin(angles)
    hi = t.astype(jnp.bfloat16)
    lo = (t - hi.astype(np.float64)).astype(jnp.bfloat16)
    hi, lo = jnp.asarray(hi), jnp.asarray(lo)
    left = jnp.concatenate([hi, hi, lo, lo], axis=1)
    zero = jnp.zeros_like(hi)
    two = lambda m: jnp.concatenate([jnp.concatenate([m, zero], 1), jnp.concatenate([zero, m], 1)], 0)
    wide = jnp.concatenate([two(hi), two(lo)], axis=1)
    right = jnp.concatenate([wide, wide], axis=0)
    return left, right

def green_table():
    p = jnp.arange(GRID, dtype=jnp.int32)
    f = jnp.minimum(p, GRID - p)
    sq = (f * f).astype(jnp.float32)
    tot = sq[:, None, None] + sq[None, :, None] + jnp.concatenate([sq, sq])[None, None, :]
    c = box_length**2 / (math.pi * GRID**3)
    return jnp.where(tot > 0.5, c / jnp.maximum(tot, 1.0), 0.0)

def dot(a, b):
    return jnp.dot(a, b, preferred_element_type=jnp.float32)

def along_lanes(x, right):
    hi, lo = split(x)
    y = dot(jnp.concatenate([hi, lo], axis=1), right)
    return y[:, :128] + y[:, 128:]

def along_rows(left, x):
    hi, lo = split(x)
    return dot(left, jnp.concatenate([hi, lo, hi, lo], axis=0))

def solve_kernel(place_ref, row_ref, c0_ref, c1_ref, c2_ref, c3_ref, left_ref, right_ref, green_ref, out_ref, f_ref):
    zp = place_ref[0]
    left = left_ref[...]
    right = right_ref[...]
    low = lax.broadcasted_iota(jnp.int32, (GRID, 128), 1) < 64

    def column(ref, lanes):
        return jnp.concatenate([ref[lax.rem(zp - b + 8, 8), :, lanes] for b in range(8)], axis=0).astype(jnp.float32)

    for pack, (a_ref, b_ref) in enumerate(((c0_ref, c1_ref), (c2_ref, c3_ref))):
        def forward(step, _):
            packed = []
            for i in range(GF):
                yh = step * GF + i
                lanes = pl.ds(pl.multiple_of(yh * 128, 128), 128)
                row = row_ref[:, lanes].astype(jnp.float32)
                d1 = row * column(a_ref, lanes)
                d2 = row * column(b_ref, lanes)
                packed.append(jnp.where(low, d1, pltpu.roll(d2, 64, 1)))
                packed.append(jnp.where(low, pltpu.roll(d1, 64, 1), d2))
            g = along_lanes(jnp.concatenate(packed, axis=0), right)
            h = along_rows(left, jnp.concatenate([g[64 * i:64 * i + 64] for i in range(2 * GF)], axis=1))
            f_ref[pl.ds(pl.multiple_of(step * (128 * GF), 128 * GF), 128 * GF), :] = jnp.concatenate([h[:, 128 * i:128 * i + 128] for i in range(2 * GF)], axis=0)
            return 0
        lax.fori_loop(0, 32 // GF, forward, 0)

        def middle(kk, _):
            kx = kk * GM
            g = jnp.concatenate([f_ref[pl.ds(kx + i, 64, stride=64), :] for i in range(GM)], axis=1)
            h = along_rows(left, g)
            h = h * jnp.concatenate([green_ref[kx + i] for i in range(GM)], axis=1)
            u = along_rows(left, h)
            for i in range(GM):
                f_ref[pl.ds(kx + i, 64, stride=64), :] = u[:, 128 * i:128 * i + 128]
            return 0
        lax.fori_loop(0, 64 // GM, middle, 0)

        occ_a = a_ref[0, :, 4096:4224].astype(jnp.float32)[0:1, :]
        occ_b = b_ref[0, :, 4096:4224].astype(jnp.float32)[0:1, :]

        def backward(step, _):
            h = f_ref[pl.ds(pl.multiple_of(step * (128 * GF), 128 * GF), 128 * GF), :]
            g = along_rows(left, jnp.concatenate([h[64 * i:64 * i + 64] for i in range(2 * GF)], axis=1))
            p = along_lanes(jnp.concatenate([g[:, 128 * i:128 * i + 128] for i in range(2 * GF)], axis=0), right)
            for i in range(GF):
                yh = step * GF + i
                lanes = pl.ds(pl.multiple_of(yh * 128, 128), 128)
                p0, p1 = p[128 * i:128 * i + 64], p[128 * i + 64:128 * i + 128]
                v1 = jnp.where(low, p0, pltpu.roll(p1, 64, 1))
                v2 = jnp.where(low, pltpu.roll(p0, 64, 1), p1)
                term = v1 * (column(a_ref, lanes) * occ_a) + v2 * (column(b_ref, lanes) * occ_b)
                if pack:
                    term = out_ref[:, lanes] + term
                out_ref[:, lanes] = term
            return 0
        lax.fori_loop(0, 32 // GF, backward, 0)

def solve(place, row, c0, c1, c2, c3, left, right, green):
    vm = pl.BlockSpec(memory_space=pltpu.VMEM)
    return pl.pallas_call(
        solve_kernel,
        out_shape=jax.ShapeDtypeStruct((GRID, GRID * GRID), jnp.float32),
        in_specs=[pl.BlockSpec(memory_space=pltpu.SMEM)] + [vm] * 8,
        out_specs=vm,
        scratch_shapes=[pltpu.VMEM((GRID * GRID, 128), jnp.float32)],
        name="solve",
    )(place, row, c0, c1, c2, c3, left, right, green)


AXES = ("grp", "dist")


def device(half, z, core, lane):
    return ((half * 8 + z) * 2 + core) * 8 + lane


def moved(x, rule):
    pairs = [
        (device(h, z, c, l), device(*rule(h, z, c, l)))
        for h in range(2)
        for z in range(8)
        for c in range(2)
        for l in range(8)
    ]
    return lax.ppermute(x, AXES, pairs)


def body(orbitals, occupations):
    mine = orbitals[0]
    copies = jnp.broadcast_to(mine, (8, *mine.shape))
    row = lax.all_to_all(copies, "dist", split_axis=0, concat_axis=0, tiled=True)
    row = row.reshape(GRID, GRID * GRID)
    weight = jnp.broadcast_to(occupations[0], (mine.shape[0], 128))
    slice_out = jnp.concatenate([mine, weight], axis=1)
    pieces = [
        moved(slice_out, lambda h, z, c, l, k=k: (h, (l + k) % 8, c, z)) for k in range(8)
    ]
    col = jnp.stack(pieces)
    core_col = moved(col, lambda h, z, c, l: (h, z, 1 - c, l))
    far_col = moved(col, lambda h, z, c, l: (1 - h, z, c, l))
    far_core_col = moved(far_col, lambda h, z, c, l: (h, z, 1 - c, l))
    place = (lax.axis_index("grp") // 2 % 8).astype(jnp.int32).reshape(1)
    left, right = tables()
    partial = solve(place, row, col, core_col, far_col, far_core_col, left, right, green_table())
    arrived = lax.all_to_all(
        partial.reshape(8, 8, GRID * GRID), "dist", split_axis=0, concat_axis=0, tiled=True
    )
    return -arrived.sum(axis=0)[None]


def solution(mesh):
    in_specs = (P("grp", "dist", None), P("grp"))
    out_specs = P("grp", "dist", None)
    return jax.shard_map(body, mesh=mesh, in_specs=in_specs, out_specs=out_specs, check_vma=False)
```

time: 443 us -> 114 us (0.26)
  waiting for transfers between devices: 141 us -> 18.2 us
  blocking collectives: 90.6 us -> 18.8 us
  local copies, waits for them, and re-layouts: 56.5 us -> 3.75 us
  matrix products: 51.7 us -> 0 us
  Pallas kernels: 0 us -> 22.2 us
  other arithmetic: 17.4 us -> 2.58 us
  between operations: 15.1 us -> 0.79 us
  loops' own time: 12.3 us -> 0 us
  starting transfers between devices: 53.5 us -> 46.2 us
    reduce_scatter x1 -> x0, waiting for transfers between devices: 102 us -> none  [body(): lax.psum_scatter(placed.reshape(groups * members, planes, GRID * GRID), '...]
    unnamed x1 -> x0, blocking collectives: 72.2 us -> none
    dot_general x12 -> x0, matrix products: 51.7 us -> none  [the longest x4 24.2 us: full_solver(): field = jnp.einsum('pxyz,wz->pxyw', field, table, precision=highest)]
    all_to_all x3 -> x1, starting transfers between devices: 53.4 us -> 9.76 us  [body(): lax.all_to_all(copies, 'dist', split_axis=0, concat_axis=0, tiled=True)]
    ppermute x0 -> x11, starting transfers between devices: none -> 36.5 us  [moved(): return lax.ppermute(x, AXES, pairs)]
    all_to_all x3 -> x1, waiting for transfers between devices: 35.2 us -> 9.31 us  [body(): lax.all_to_all(copies, 'dist', split_axis=0, concat_axis=0, tiled=True)]
    pallas_call x0 -> x1, Pallas kernels: none -> 22.2 us  [solve(): pl.pallas_call(solve_kernel, out_shape=jax.ShapeDtypeStruct((GRID, GRID *...]
    broadcast_in_dim x3 -> x1, local copies, waits for them, and re-layouts: 19.4 us -> 1.68 us  [body(): copies = jnp.broadcast_to(mine, (8, *mine.shape))]
  transfers between devices with their start and end apart: 5 -> 12, of which waited for: 4 -> 4; matrix products, arithmetic and copies ran while one was open for 3% -> 3% of each run, Pallas kernels for 0% -> 0%
where the time goes in v1:
time: 114 us; the launch traced here: 113 us
  starting transfers between devices  46.2 us (41%)
  Pallas kernels  22.2 us (19%)
  blocking collectives  18.8 us (16%)
  waiting for transfers between devices  18.2 us (16%)
  local copies, waits for them, and re-layouts  3.75 us (3%)
  other arithmetic  2.58 us (2%)
    ppermute x11, starting transfers between devices, moved(): return lax.ppermute(x, AXES, pairs)  36.5 us
    pallas_call x1, Pallas kernels, solve(): pl.pallas_call(solve_kernel, out_shape=jax.ShapeDtypeStruct((GRID, GRID *...  22.2 us
    all_to_all x1, blocking collectives, body(): lax.all_to_all(partial.reshape(8, 8, GRID * GRID), 'dist', split_axis=0,...  18.8 us
    all_to_all x1, starting transfers between devices, body(): lax.all_to_all(copies, 'dist', split_axis=0, concat_axis=0, tiled=True)  9.76 us
    all_to_all x1, waiting for transfers between devices, body(): lax.all_to_all(copies, 'dist', split_axis=0, concat_axis=0, tiled=True)  9.31 us
    ppermute x11, waiting for transfers between devices, moved(): return lax.ppermute(x, AXES, pairs)  8.92 us
  transfers between devices with their start and end apart: 12, of which 4 were waited for; matrix products, arithmetic and copies ran while one was open for 3% of the time, Pallas kernels for 0%

profile of v1, /device:TPU:8, one launch (start us, length us, event | category | flops | bytes accessed | tf_op | source)
XLA Modules:
  0.0 112.5 jit_solution(2478821414630054499)
XLA Ops:
  0.7 0.8 concatenate.33
  1.5 5.1 %collective-permute-start = (bf16[8,4224]{1,0:T(8,128)(2,1)S(1)}, bf16[8,4224]{1,0:T(8,128)(2,1)S(1)}, u32[]{:S(2)}, u32[]{:S(2)}) collective-permute-start(bf16[8,4224]{1,0:T(8,128)(2,1)S(1)} %concatenate.33), channel_id=1, source_target_pairs={{0,0},{1,16},{2,32},{3,48},{4,64},{5,80},{6,96},{7,112},{8,8},{9,2... | collective-permute-start | bytes 202760 | tf_op jit(solution)/shard_map/ppermute | solution.py:138
  6.7 3.9 %collective-permute-start.6 = (bf16[8,4224]{1,0:T(8,128)(2,1)S(1)}, bf16[8,4224]{1,0:T(8,128)(2,1)S(1)}, u32[]{:S(2)}, u32[]{:S(2)}) collective-permute-start(bf16[8,4224]{1,0:T(8,128)(2,1)S(1)} %concatenate.33), channel_id=1, source_target_pairs={{0,96},{1,112},{2,0},{3,16},{4,32},{5,48},{6,64},{7,80},{8,104},{9... | collective-permute-start | bytes 202760 | tf_op jit(solution)/shard_map/ppermute | solution.py:138
  10.6 4.1 %collective-permute-start.5 = (bf16[8,4224]{1,0:T(8,128)(2,1)S(1)}, bf16[8,4224]{1,0:T(8,128)(2,1)S(1)}, u32[]{:S(2)}, u32[]{:S(2)}) collective-permute-start(bf16[8,4224]{1,0:T(8,128)(2,1)S(1)} %concatenate.33), channel_id=1, source_target_pairs={{0,80},{1,96},{2,112},{3,0},{4,16},{5,32},{6,48},{7,64},{8,88},{9,... | collective-permute-start | bytes 202760 | tf_op jit(solution)/shard_map/ppermute | solution.py:138
  14.7 1.6 %collective-permute-start.4 = (bf16[8,4224]{1,0:T(8,128)(2,1)S(1)}, bf16[8,4224]{1,0:T(8,128)(2,1)S(1)}, u32[]{:S(2)}, u32[]{:S(2)}) collective-permute-start(bf16[8,4224]{1,0:T(8,128)(2,1)S(1)} %concatenate.33), channel_id=1, source_target_pairs={{0,64},{1,80},{2,96},{3,112},{4,0},{5,16},{6,32},{7,48},{8,72},{9,... | collective-permute-start | bytes 202760 | tf_op jit(solution)/shard_map/ppermute | solution.py:138
  16.3 8.2 %collective-permute-start.1 = (bf16[8,4224]{1,0:T(8,128)(2,1)S(1)}, bf16[8,4224]{1,0:T(8,128)(2,1)S(1)}, u32[]{:S(2)}, u32[]{:S(2)}) collective-permute-start(bf16[8,4224]{1,0:T(8,128)(2,1)S(1)} %concatenate.33), channel_id=1, source_target_pairs={{0,16},{1,32},{2,48},{3,64},{4,80},{5,96},{6,112},{7,0},{8,24},{9,... | collective-permute-start | bytes 202760 | tf_op jit(solution)/shard_map/ppermute | solution.py:138
  24.6 3.3 %collective-permute-done.1 = bf16[8,4224]{1,0:T(8,128)(2,1)S(1)} collective-permute-done((bf16[8,4224]{1,0:T(8,128)(2,1)S(1)}, bf16[8,4224]{1,0:T(8,128)(2,1)S(1)}, u32[]{:S(2)}, u32[]{:S(2)}) %collective-permute-start.1) | collective-permute-done | bytes 67616 | tf_op jit(solution)/shard_map/ppermute | solution.py:138
  27.9 4.4 %collective-permute-start.2 = (bf16[8,4224]{1,0:T(8,128)(2,1)S(1)}, bf16[8,4224]{1,0:T(8,128)(2,1)S(1)}, u32[]{:S(2)}, u32[]{:S(2)}) collective-permute-start(bf16[8,4224]{1,0:T(8,128)(2,1)S(1)} %concatenate.33), channel_id=1, source_target_pairs={{0,32},{1,48},{2,64},{3,80},{4,96},{5,112},{6,0},{7,16},{8,40},{9,... | collective-permute-start | bytes 202760 | tf_op jit(solution)/shard_map/ppermute | solution.py:138
  32.2 3.7 %collective-permute-done.2 = bf16[8,4224]{1,0:T(8,128)(2,1)S(1)} collective-permute-done((bf16[8,4224]{1,0:T(8,128)(2,1)S(1)}, bf16[8,4224]{1,0:T(8,128)(2,1)S(1)}, u32[]{:S(2)}, u32[]{:S(2)}) %collective-permute-start.2) | collective-permute-done | bytes 67616 | tf_op jit(solution)/shard_map/ppermute | solution.py:138
  35.9 5.7 %collective-permute-start.3 = (bf16[8,4224]{1,0:T(8,128)(2,1)S(1)}, bf16[8,4224]{1,0:T(8,128)(2,1)S(1)}, u32[]{:S(2)}, u32[]{:S(2)}) collective-permute-start(bf16[8,4224]{1,0:T(8,128)(2,1)S(1)} %concatenate.33), channel_id=1, source_target_pairs={{0,48},{1,64},{2,80},{3,96},{4,112},{5,0},{6,16},{7,32},{8,56},{9,... | collective-permute-start | bytes 202760 | tf_op jit(solution)/shard_map/ppermute | solution.py:138
  41.6 1.9 %collective-permute-done.3 = bf16[8,4224]{1,0:T(8,128)(2,1)S(1)} collective-permute-done((bf16[8,4224]{1,0:T(8,128)(2,1)S(1)}, bf16[8,4224]{1,0:T(8,128)(2,1)S(1)}, u32[]{:S(2)}, u32[]{:S(2)}) %collective-permute-start.3) | collective-permute-done | bytes 67616 | tf_op jit(solution)/shard_map/ppermute | solution.py:138
  43.7 2.8 %collective-permute-start.9 = (bf16[8,8,4224]{2,1,0:T(8,128)(2,1)S(1)}, bf16[8,8,4224]{2,1,0:T(8,128)(2,1)S(1)}, u32[]{:S(2)}, u32[]{:S(2)}) collective-permute-start(bf16[8,8,4224]{2,1,0:T(8,128)(2,1)S(1)} %bitcast_dynamic-update-slice_fusion.c0_ref), channel_id=1, source_target_pairs={{0,128},{1,129},{2,130},{3,131},{4,132},{5,133},{6,134},{7,135},{8... | collective-permute-start | bytes 1622024 | tf_op jit(solution)/shard_map/ppermute | solution.py:138
  46.5 1.7 %broadcast_in_dim.5 = bf16[8,8,4096]{2,1,0:T(8,128)(2,1)} broadcast(bf16[8,4096]{1,0:T(8,128)(2,1)} %bitcast.27), dimensions={1,2} | broadcast | bytes 589824 | tf_op jit(solution)/shard_map/broadcast_in_dim | solution.py:143
  48.1 9.8 %all-to-all-start = ((bf16[8,8,4096]{2,1,0:T(8,128)(2,1)}), bf16[8,8,4096]{2,1,0:T(8,128)(2,1)S(1)}, u32[]{:S(2)}, u32[]{:S(2)}) async-start(bf16[8,8,4096]{2,1,0:T(8,128)(2,1)} %broadcast_in_dim.5), calls=%async_computation | async-start | bytes 1048576 | tf_op jit(solution)/shard_map/all_to_all | solution.py:144
  57.9 0.1 collective-permute-start.8
  58.0 0.5 collective-permute-start.10
  58.7 1.7 %fusion.1.green_ref = f32[64,64,128]{2,1,0:T(8,128)} fusion(f32[128]{0:T(128)S(1)} %pad_maximum_fusion, f32[64,64]{1,0:T(8,128)S(1)} %broadcast_add_fusion), kind=kLoop, calls=%fused_computation.3 | loop fusion | flops 2621440 | bytes 2114048 | tf_op jit(solution)/shard_map/jit(_where)/select_n | solution.py:40
  60.4 9.3 %all-to-all-done = bf16[8,8,4096]{2,1,0:T(8,128)(2,1)S(1)} async-done(((bf16[8,8,4096]{2,1,0:T(8,128)(2,1)}), bf16[8,8,4096]{2,1,0:T(8,128)(2,1)S(1)}, u32[]{:S(2)}, u32[]{:S(2)}) %all-to-all-start) | async-done | bytes 524320 | tf_op jit(solution)/shard_map/all_to_all | solution.py:144
  69.7 0.8 copy-done
  70.5 0.1 copy-done.3
  70.6 0.2 copy-done.4
  70.8 22.2 %solve.1 = f32[64,4096]{1,0:T(8,128)} custom-call(s32[1]{0:T(128)} %bitcast.place_ref, bf16[64,4096]{1,0:T(8,128)(2,1)} %bitcast.25, bf16[8,8,4224]{2,1,0:T(8,128)(2,1)} %copy-done.1, bf16[8,8,4224]{2,1,0:T(8,128)(2,1)} %copy-done.3, bf16[8,8,4224]{2,1,0:T(8,128)(2,1)} %copy-done.2, bf16[8,8,4224]{2,1,0:T(8,128)(2,1)} %copy-done.4, ...), custom_call_target="tpu_custom_call" | custom-call | tf_op jit(solution)/shard_map/solve/pallas_call | solution.py:113
  93.0 18.8 %all_to_all.10 = f32[8,8,4096]{2,1,0:T(8,128)S(1)} all-to-all(f32[8,8,4096]{2,1,0:T(8,128)} %bitcast.24), channel_id=1, replica_groups=mesh['grp'=32,'dist'=8] {'dist'}, dimensions={0} | all-to-all | bytes 2097152 | tf_op jit(solution)/shard_map/all_to_all | solution.py:158
  111.8 0.7 negate_bitcast_fusion
  (28 shorter events, 0.4 us)
Async XLA Ops:
  1.5 14.8 %collective-permute-start = (bf16[8,4224]{1,0:T(8,128)(2,1)S(1)}, bf16[8,4224]{1,0:T(8,128)(2,1)S(1)}, u32[]{:S(2)}, u32[]{:S(2)}) collective-permute-start(bf16[8,4224]{1,0:T(8,128)(2,1)S(1)} %concatenate.33), channel_id=1, source_target_pairs={{0,0},{1,16},{2,32},{3,48},{4,64},{5,80},{6,96},{7,112},{8,8},{9,2... | collective-permute-start | bytes 202760 | tf_op jit(solution)/shard_map/ppermute | solution.py:138
  6.6 37.1 %collective-permute-start.7 = (bf16[8,4224]{1,0:T(8,128)(2,1)S(1)}, bf16[8,4224]{1,0:T(8,128)(2,1)S(1)}, u32[]{:S(2)}, u32[]{:S(2)}) collective-permute-start(bf16[8,4224]{1,0:T(8,128)(2,1)S(1)} %concatenate.33), channel_id=1, source_target_pairs={{0,112},{1,0},{2,16},{3,32},{4,48},{5,64},{6,80},{7,96},{8,120},{9... | collective-permute-start | bytes 202760 | tf_op jit(solution)/shard_map/ppermute | solution.py:138
  6.7 36.9 %collective-permute-start.6 = (bf16[8,4224]{1,0:T(8,128)(2,1)S(1)}, bf16[8,4224]{1,0:T(8,128)(2,1)S(1)}, u32[]{:S(2)}, u32[]{:S(2)}) collective-permute-start(bf16[8,4224]{1,0:T(8,128)(2,1)S(1)} %concatenate.33), channel_id=1, source_target_pairs={{0,96},{1,112},{2,0},{3,16},{4,32},{5,48},{6,64},{7,80},{8,104},{9... | collective-permute-start | bytes 202760 | tf_op jit(solution)/shard_map/ppermute | solution.py:138
  10.6 33.0 %collective-permute-start.5 = (bf16[8,4224]{1,0:T(8,128)(2,1)S(1)}, bf16[8,4224]{1,0:T(8,128)(2,1)S(1)}, u32[]{:S(2)}, u32[]{:S(2)}) collective-permute-start(bf16[8,4224]{1,0:T(8,128)(2,1)S(1)} %concatenate.33), channel_id=1, source_target_pairs={{0,80},{1,96},{2,112},{3,0},{4,16},{5,32},{6,48},{7,64},{8,88},{9,... | collective-permute-start | bytes 202760 | tf_op jit(solution)/shard_map/ppermute | solution.py:138
  14.7 28.9 %collective-permute-start.4 = (bf16[8,4224]{1,0:T(8,128)(2,1)S(1)}, bf16[8,4224]{1,0:T(8,128)(2,1)S(1)}, u32[]{:S(2)}, u32[]{:S(2)}) collective-permute-start(bf16[8,4224]{1,0:T(8,128)(2,1)S(1)} %concatenate.33), channel_id=1, source_target_pairs={{0,64},{1,80},{2,96},{3,112},{4,0},{5,16},{6,32},{7,48},{8,72},{9,... | collective-permute-start | bytes 202760 | tf_op jit(solution)/shard_map/ppermute | solution.py:138
  16.3 11.5 %collective-permute-start.1 = (bf16[8,4224]{1,0:T(8,128)(2,1)S(1)}, bf16[8,4224]{1,0:T(8,128)(2,1)S(1)}, u32[]{:S(2)}, u32[]{:S(2)}) collective-permute-start(bf16[8,4224]{1,0:T(8,128)(2,1)S(1)} %concatenate.33), channel_id=1, source_target_pairs={{0,16},{1,32},{2,48},{3,64},{4,80},{5,96},{6,112},{7,0},{8,24},{9,... | collective-permute-start | bytes 202760 | tf_op jit(solution)/shard_map/ppermute | solution.py:138
  27.9 8.0 %collective-permute-start.2 = (bf16[8,4224]{1,0:T(8,128)(2,1)S(1)}, bf16[8,4224]{1,0:T(8,128)(2,1)S(1)}, u32[]{:S(2)}, u32[]{:S(2)}) collective-permute-start(bf16[8,4224]{1,0:T(8,128)(2,1)S(1)} %concatenate.33), channel_id=1, source_target_pairs={{0,32},{1,48},{2,64},{3,80},{4,96},{5,112},{6,0},{7,16},{8,40},{9,... | collective-permute-start | bytes 202760 | tf_op jit(solution)/shard_map/ppermute | solution.py:138
  35.9 7.6 %collective-permute-start.3 = (bf16[8,4224]{1,0:T(8,128)(2,1)S(1)}, bf16[8,4224]{1,0:T(8,128)(2,1)S(1)}, u32[]{:S(2)}, u32[]{:S(2)}) collective-permute-start(bf16[8,4224]{1,0:T(8,128)(2,1)S(1)} %concatenate.33), channel_id=1, source_target_pairs={{0,48},{1,64},{2,80},{3,96},{4,112},{5,0},{6,16},{7,32},{8,56},{9,... | collective-permute-start | bytes 202760 | tf_op jit(solution)/shard_map/ppermute | solution.py:138
  43.7 26.0 %copy-start.1 = (bf16[8,8,4224]{2,1,0:T(8,128)(2,1)}, bf16[8,8,4224]{2,1,0:T(8,128)(2,1)S(1)}, u32[]{:S(2)}) copy-start(bf16[8,8,4224]{2,1,0:T(8,128)(2,1)S(1)} %bitcast_dynamic-update-slice_fusion.c0_ref) | copy-start | bytes 1622020
  43.7 14.3 %collective-permute-start.9 = (bf16[8,8,4224]{2,1,0:T(8,128)(2,1)S(1)}, bf16[8,8,4224]{2,1,0:T(8,128)(2,1)S(1)}, u32[]{:S(2)}, u32[]{:S(2)}) collective-permute-start(bf16[8,8,4224]{2,1,0:T(8,128)(2,1)S(1)} %bitcast_dynamic-update-slice_fusion.c0_ref), channel_id=1, source_target_pairs={{0,128},{1,129},{2,130},{3,131},{4,132},{5,133},{6,134},{7,135},{8... | collective-permute-start | bytes 1622024 | tf_op jit(solution)/shard_map/ppermute | solution.py:138
  48.1 21.5 %all-to-all-start = ((bf16[8,8,4096]{2,1,0:T(8,128)(2,1)}), bf16[8,8,4096]{2,1,0:T(8,128)(2,1)S(1)}, u32[]{:S(2)}, u32[]{:S(2)}) async-start(bf16[8,8,4096]{2,1,0:T(8,128)(2,1)} %broadcast_in_dim.5), calls=%async_computation | async-start | bytes 1048576 | tf_op jit(solution)/shard_map/all_to_all | solution.py:144
  57.9 11.8 %collective-permute-start.8 = (bf16[8,8,4224]{2,1,0:T(8,128)(2,1)S(1)}, bf16[8,8,4224]{2,1,0:T(8,128)(2,1)S(1)}, u32[]{:S(2)}, u32[]{:S(2)}) collective-permute-start(bf16[8,8,4224]{2,1,0:T(8,128)(2,1)S(1)} %bitcast_dynamic-update-slice_fusion.c0_ref), channel_id=1, source_target_pairs={{0,8},{1,9},{2,10},{3,11},{4,12},{5,13},{6,14},{7,15},{8,0},{9,1},... | collective-permute-start | bytes 1622024 | tf_op jit(solution)/shard_map/ppermute | solution.py:138
  58.0 11.7 %copy-start.2 = (bf16[8,8,4224]{2,1,0:T(8,128)(2,1)}, bf16[8,8,4224]{2,1,0:T(8,128)(2,1)S(1)}, u32[]{:S(2)}) copy-start(bf16[8,8,4224]{2,1,0:T(8,128)(2,1)S(1)} %collective-permute-done.9.c2_ref) | copy-start | bytes 1622020
  58.0 11.6 %collective-permute-start.10 = (bf16[8,8,4224]{2,1,0:T(8,128)(2,1)S(1)}, bf16[8,8,4224]{2,1,0:T(8,128)(2,1)S(1)}, u32[]{:S(2)}, u32[]{:S(2)}) collective-permute-start(bf16[8,8,4224]{2,1,0:T(8,128)(2,1)S(1)} %collective-permute-done.9.c2_ref), channel_id=1, source_target_pairs={{0,8},{1,9},{2,10},{3,11},{4,12},{5,13},{6,14},{7,15},{8,0},{9,1},... | collective-permute-start | bytes 1622024 | tf_op jit(solution)/shard_map/ppermute | solution.py:138
  69.7 0.8 copy-start
  69.7 1.0 copy-start.3
  69.7 1.1 %copy-start.4 = (bf16[8,8,4224]{2,1,0:T(8,128)(2,1)}, bf16[8,8,4224]{2,1,0:T(8,128)(2,1)S(1)}, u32[]{:S(2)}) copy-start(bf16[8,8,4224]{2,1,0:T(8,128)(2,1)S(1)} %collective-permute-done.10.c3_ref) | copy-start | bytes 1622020
